TPU v7x, 128 devices: a whole 4x4x4 slice. The times are simulated.
128 devices in a mesh: pix: 32 (over y, z, core), freq: 4 (over x).
Axes of the slice: x: 4, y: 4, z: 4, core: 2. Of those that a mesh axis runs over, the one named last changes fastest.
Arguments:
- cube: float32 [1024, 65536], P('freq', 'pix'), may hold values from -6 to 6
- probes: float32 [32, 65536], P(None, 'pix'), may hold values from -6 to 6
- galaxy: float32 [65536], P('pix'), may hold values from -6 to 6
- slices: int32 [65536], P('pix'), may hold values from 0 to 127
- valid: int32 [65536], P('pix'), may hold values 0 or 1
Outputs:
- cleaned: float32 [1024, 65536], P('freq', 'pix')
- cross: float32 [1024, 128], P('freq')
All inputs are finite; a program needn't handle non-finite values. No bound on the sum of `valid` on one device may be relied on, other than what follows from the above.
Results may differ from a plain program's by a relative error of at most 0.00019.
Values sent between devices are 32-bit elements; how exact they have to be, the bound alone decides.
No kernel may reach another device: no remote copies, remote signals or barrier semaphores. Data moves between devices by JAX's collectives and lax.ppermute only.
A program may use at most 64 MiB of HBM per device.

v0:
```python
import jax
import jax.numpy as jnp
from jax import lax
from jax.sharding import PartitionSpec as P

NS = 128
ITERS = 4


def prefix(value, axis, join, neutral):
    count, mine = (lax.axis_size(axis), lax.axis_index(axis))
    pieces = lax.all_gather(value, axis)
    total = jnp.full_like(value, 0) + jnp.asarray(neutral, value.dtype)

    def lap(position, total):
        longer = join(total, pieces[position])
        return jnp.where(position < mine, longer, total)

    return lax.fori_loop(0, count - 1, lap, total)


def broadcast(value, axis, source):
    kept = jnp.where(lax.axis_index(axis) == source, value, 0).astype(value.dtype)
    return lax.psum(kept, axis)


def multiply(left, right):
    return jnp.dot(left, right, precision=lax.Precision.HIGHEST, preferred_element_type=jnp.float32)


def orthonormal(factor):
    gram = multiply(factor.T, factor)
    lower = jnp.linalg.cholesky(gram)
    return lax.linalg.triangular_solve(lower, factor, left_side=False, lower=True, transpose_a=True)


def combine_add(earlier, later):
    return earlier + later


def total_pix(term):
    before = prefix(term, "pix", combine_add, jnp.zeros_like(term))
    return broadcast(before + term, "pix", lax.axis_size("pix") - 1)


def fold_freq(term):
    return lax.psum_scatter(term, "freq", scatter_dimension=0, tiled=True)


def gather_rows(term):
    return lax.all_gather(term, "freq", axis=0, tiled=True)


def slice_table(slices, weights):
    levels = jnp.arange(NS, dtype=jnp.int32)
    return (slices[:, None] == levels[None, :]).astype(jnp.float32) * weights[:, None]


def body(cube, probes, galaxy, slices, valid):
    pixels = lax.axis_size("pix") * cube.shape[1]
    factor_scale = (float(pixels) / float(NS)) ** (-0.5)
    weights = galaxy * valid.astype(jnp.float32)
    own = lax.axis_index("freq")
    local = lax.all_to_all(cube, "freq", split_axis=1, concat_axis=0, tiled=True)
    width = local.shape[1]
    start = own * width
    probe_cols = lax.dynamic_slice_in_dim(probes, start, width, 1)
    own_weights = lax.dynamic_slice_in_dim(weights, start, width, 0)
    own_slices = lax.dynamic_slice_in_dim(slices, start, width, 0)
    basis = orthonormal(gather_rows(total_pix(fold_freq(multiply(local, probe_cols.T)))))
    for step in range(ITERS):
        amps = multiply(basis.T, local)
        basis = orthonormal(gather_rows(total_pix(fold_freq(multiply(local, amps.T)))))
    amps = multiply(basis.T, local)
    cleaned_local = local - multiply(basis, amps)
    table = slice_table(own_slices, own_weights)
    cross = total_pix(fold_freq(multiply(cleaned_local, table))) * factor_scale
    cleaned = lax.all_to_all(cleaned_local, "freq", split_axis=0, concat_axis=1, tiled=True)
    return (cleaned, cross)


def solution(mesh):
    in_specs = (P("freq", "pix"), P(None, "pix"), P("pix"), P("pix"), P("pix"))
    out_specs = (P("freq", "pix"), P("freq", None))
    return jax.shard_map(body, mesh=mesh, in_specs=in_specs, out_specs=out_specs, check_vma=False)
```

profile of v0, /device:TPU:1, one launch (start us, length us, event | category | flops | bytes accessed | tf_op | source)
XLA Modules:
  0.0 1482.5 jit_solution(6170851042177497390)
XLA Ops:
  7.2 3.2 copy.32
  10.4 4.8 all-to-all-start
  15.2 25.5 %all-to-all-done = f32[256,4,512]{2,0,1:T(8,128)S(1)} async-done(((f32[256,4,512]{2,0,1:T(8,128)}), f32[256,4,512]{2,0,1:T(8,128)S(1)}, u32[]{:S(2)}, u32[]{:S(2)}) %all-to-all-start) | async-done | bytes 2097184 | tf_op jit(solution)/shard_map/all_to_all | solution.py:64
  40.7 2.7 convolution_bitcast_fusion.9
  43.4 20.1 %reduce-scatter.7.cloned.1.call-done = f32[256,32]{0,1:T(8,128)} async-done(((f32[1024,32]{0,1:T(8,128)}), f32[256,32]{0,1:T(8,128)}) %reduce-scatter.7.cloned.1.call-update) | async-done | bytes 32784 | tf_op jit(solution)/shard_map/reduce_scatter | solution.py:47
  63.6 47.6 %all-gather.13.cloned.1.call-done = f32[8192,32]{0,1:T(8,128)} async-done(((f32[256,32]{0,1:T(8,128)}), f32[8192,32]{0,1:T(8,128)}) %all-gather.13.cloned.1.call-update) | async-done | bytes 1048592 | tf_op jit(solution)/shard_map/all_gather | solution.py:12
  111.1 3.6 copy.24
  114.7 30.1 %while.84 = (s32[]{:T(128)}, f32[256,32]{1,0:T(8,128)S(1)}, s32[]{:T(128)}, f32[32,256,32]{2,1,0:T(8,128)}, s32[]{:T(128)}, /*index=5*/s32[]{:T(128)}) while((s32[]{:T(128)}, f32[256,32]{1,0:T(8,128)S(1)}, s32[]{:T(128)}, f32[32,256,32]{2,1,0:T(8,128)}, s32[]{:T(128)}, /*index=5*/s32[]{:T(128)}) %tuple.222), condition=%wide.region_2.3_spmd.clone, body=%wide.region_1.2_spmd.clone.sunk | while | flops 24580 | bytes 98397 | solution.py:19
  144.9 120.9 %psum.42 = f32[256,32]{0,1:T(8,128)S(1)} all-reduce(f32[256,32]{0,1:T(8,128)S(1)} %add_select_fusion.11), channel_id=1, replica_groups=mesh['pix'=32,'freq'=4] {'pix'}, use_global_device_ids=true, to_apply=%region_3.4 | all-reduce | flops 8192 | bytes 65536 | tf_op jit(solution)/shard_map/psum | solution.py:24
  265.7 9.7 all_gather.53
  275.8 2.9 cholesky.89
  280.0 2.4 custom-call.15
  282.8 1.3 fusion.32
  284.1 2.7 convolution_bitcast_fusion.7
  286.8 21.6 %reduce-scatter.9.cloned.1.call-done = f32[256,32]{0,1:T(8,128)} async-done(((f32[1024,32]{0,1:T(8,128)}), f32[256,32]{0,1:T(8,128)}) %reduce-scatter.9.cloned.1.call-update) | async-done | bytes 32784 | tf_op jit(solution)/shard_map/reduce_scatter | solution.py:47
  308.6 47.4 %all-gather.15.cloned.1.call-done = f32[8192,32]{0,1:T(8,128)} async-done(((f32[256,32]{0,1:T(8,128)}), f32[8192,32]{0,1:T(8,128)}) %all-gather.15.cloned.1.call-update) | async-done | bytes 1048592 | tf_op jit(solution)/shard_map/all_gather | solution.py:12
  356.0 3.6 copy.25
  359.5 30.1 %while.85 = (s32[]{:T(128)}, f32[256,32]{1,0:T(8,128)S(1)}, s32[]{:T(128)}, f32[32,256,32]{2,1,0:T(8,128)}, s32[]{:T(128)}, /*index=5*/s32[]{:T(128)}) while((s32[]{:T(128)}, f32[256,32]{1,0:T(8,128)S(1)}, s32[]{:T(128)}, f32[32,256,32]{2,1,0:T(8,128)}, s32[]{:T(128)}, /*index=5*/s32[]{:T(128)}) %tuple.223), condition=%wide.region_8.11_spmd.clone, body=%wide.region_7.10_spmd.clone.sunk | while | flops 24580 | bytes 98397 | solution.py:19
  389.7 120.9 %psum.43 = f32[256,32]{0,1:T(8,128)S(1)} all-reduce(f32[256,32]{0,1:T(8,128)S(1)} %add_select_fusion.10), channel_id=1, replica_groups=mesh['pix'=32,'freq'=4] {'pix'}, use_global_device_ids=true, to_apply=%region_9.12 | all-reduce | flops 8192 | bytes 65536 | tf_op jit(solution)/shard_map/psum | solution.py:24
  510.6 9.7 all_gather.56
  520.6 2.9 cholesky.100
  524.8 2.4 custom-call.16
  527.6 1.3 fusion.34
  528.9 2.7 convolution_bitcast_fusion.5
  531.7 21.6 %reduce-scatter.11.cloned.1.call-done = f32[256,32]{0,1:T(8,128)} async-done(((f32[1024,32]{0,1:T(8,128)}), f32[256,32]{0,1:T(8,128)}) %reduce-scatter.11.cloned.1.call-update) | async-done | bytes 32784 | tf_op jit(solution)/shard_map/reduce_scatter | solution.py:47
  553.4 47.4 %all-gather.17.cloned.1.call-done = f32[8192,32]{0,1:T(8,128)} async-done(((f32[256,32]{0,1:T(8,128)}), f32[8192,32]{0,1:T(8,128)}) %all-gather.17.cloned.1.call-update) | async-done | bytes 1048592 | tf_op jit(solution)/shard_map/all_gather | solution.py:12
  600.8 3.6 copy.26
  604.4 30.1 %while.86 = (s32[]{:T(128)}, f32[256,32]{1,0:T(8,128)S(1)}, s32[]{:T(128)}, f32[32,256,32]{2,1,0:T(8,128)}, s32[]{:T(128)}, /*index=5*/s32[]{:T(128)}) while((s32[]{:T(128)}, f32[256,32]{1,0:T(8,128)S(1)}, s32[]{:T(128)}, f32[32,256,32]{2,1,0:T(8,128)}, s32[]{:T(128)}, /*index=5*/s32[]{:T(128)}) %tuple.224), condition=%wide.region_12.15_spmd.clone, body=%wide.region_11.14_spmd.clone.sunk | while | flops 24580 | bytes 98397 | solution.py:19
  634.5 120.9 %psum.44 = f32[256,32]{0,1:T(8,128)S(1)} all-reduce(f32[256,32]{0,1:T(8,128)S(1)} %add_select_fusion.9), channel_id=1, replica_groups=mesh['pix'=32,'freq'=4] {'pix'}, use_global_device_ids=true, to_apply=%region_13.16 | all-reduce | flops 8192 | bytes 65536 | tf_op jit(solution)/shard_map/psum | solution.py:24
  755.4 9.9 all_gather.59
  765.6 2.9 cholesky.111
  769.8 2.4 custom-call.17
  772.6 1.3 fusion.36
  773.9 2.7 convolution_bitcast_fusion.3
  776.7 21.7 %reduce-scatter.13.cloned.1.call-done = f32[256,32]{0,1:T(8,128)} async-done(((f32[1024,32]{0,1:T(8,128)}), f32[256,32]{0,1:T(8,128)}) %reduce-scatter.13.cloned.1.call-update) | async-done | bytes 32784 | tf_op jit(solution)/shard_map/reduce_scatter | solution.py:47
  798.4 47.5 %all-gather.19.cloned.1.call-done = f32[8192,32]{0,1:T(8,128)} async-done(((f32[256,32]{0,1:T(8,128)}), f32[8192,32]{0,1:T(8,128)}) %all-gather.19.cloned.1.call-update) | async-done | bytes 1048592 | tf_op jit(solution)/shard_map/all_gather | solution.py:12
  845.9 3.6 copy.27
  849.5 30.1 %while.87 = (s32[]{:T(128)}, f32[256,32]{1,0:T(8,128)S(1)}, s32[]{:T(128)}, f32[32,256,32]{2,1,0:T(8,128)}, s32[]{:T(128)}, /*index=5*/s32[]{:T(128)}) while((s32[]{:T(128)}, f32[256,32]{1,0:T(8,128)S(1)}, s32[]{:T(128)}, f32[32,256,32]{2,1,0:T(8,128)}, s32[]{:T(128)}, /*index=5*/s32[]{:T(128)}) %tuple.225), condition=%wide.region_16.19_spmd.clone, body=%wide.region_15.18_spmd.clone.sunk | while | flops 24580 | bytes 98397 | solution.py:19
  849.5 0.9 add_select_fusion.21
  879.6 120.9 %psum.45 = f32[256,32]{0,1:T(8,128)S(1)} all-reduce(f32[256,32]{0,1:T(8,128)S(1)} %add_select_fusion.8), channel_id=1, replica_groups=mesh['pix'=32,'freq'=4] {'pix'}, use_global_device_ids=true, to_apply=%region_17.20 | all-reduce | flops 8192 | bytes 65536 | tf_op jit(solution)/shard_map/psum | solution.py:24
  1000.5 9.7 all_gather.62
  1010.5 2.9 cholesky.122
  1014.8 2.4 custom-call.18
  1017.6 1.3 fusion.38
  1018.9 2.7 convolution_bitcast_fusion.1
  1021.6 21.6 %reduce-scatter.15.cloned.1.call-done = f32[256,32]{0,1:T(8,128)} async-done(((f32[1024,32]{0,1:T(8,128)}), f32[256,32]{0,1:T(8,128)}) %reduce-scatter.15.cloned.1.call-update) | async-done | bytes 32784 | tf_op jit(solution)/shard_map/reduce_scatter | solution.py:47
  1044.9 45.8 %all-gather.21.cloned.1.call-done = f32[8192,32]{0,1:T(8,128)} async-done(((f32[256,32]{0,1:T(8,128)}), f32[8192,32]{0,1:T(8,128)}) %all-gather.21.cloned.1.call-update) | async-done | bytes 1048592 | tf_op jit(solution)/shard_map/all_gather | solution.py:12
  1090.7 3.6 copy.28
  1094.3 30.1 %while.88 = (s32[]{:T(128)}, f32[256,32]{1,0:T(8,128)S(1)}, s32[]{:T(128)}, f32[32,256,32]{2,1,0:T(8,128)}, s32[]{:T(128)}, /*index=5*/s32[]{:T(128)}) while((s32[]{:T(128)}, f32[256,32]{1,0:T(8,128)S(1)}, s32[]{:T(128)}, f32[32,256,32]{2,1,0:T(8,128)}, s32[]{:T(128)}, /*index=5*/s32[]{:T(128)}) %tuple.226), condition=%wide.region_20.23_spmd.clone, body=%wide.region_19.22_spmd.clone.sunk | while | flops 24580 | bytes 98397 | solution.py:19
  1124.4 120.9 %psum.46 = f32[256,32]{0,1:T(8,128)S(1)} all-reduce(f32[256,32]{0,1:T(8,128)S(1)} %add_select_fusion.7), channel_id=1, replica_groups=mesh['pix'=32,'freq'=4] {'pix'}, use_global_device_ids=true, to_apply=%region_21.24 | all-reduce | flops 8192 | bytes 65536 | tf_op jit(solution)/shard_map/psum | solution.py:24
  1245.3 9.9 all_gather.65
  1255.6 2.9 cholesky.133
  1259.8 2.4 custom-call.19
  1262.6 1.3 fusion.40
  1263.9 1.8 convolution_subtract_fusion
  1265.8 1.3 copy-done.1
  1267.1 2.7 fusion
  1269.8 22.6 %reduce-scatter.17.cloned.1.call-done = f32[256,128]{1,0:T(8,128)} async-done(((f32[1024,128]{1,0:T(8,128)}), f32[256,128]{1,0:T(8,128)}) %reduce-scatter.17.cloned.1.call-update) | async-done | bytes 131088 | tf_op jit(solution)/shard_map/reduce_scatter | solution.py:47
  1292.4 3.6 all-to-all-start.1
  1296.1 47.1 %all-gather.23.cloned.1.call-done = f32[8192,128]{1,0:T(8,128)} async-done(((f32[256,128]{1,0:T(8,128)}), f32[8192,128]{1,0:T(8,128)}) %all-gather.23.cloned.1.call-update) | async-done | bytes 4194320 | tf_op jit(solution)/shard_map/all_gather | solution.py:12
  1343.3 30.0 %while.89 = (s32[]{:T(128)}, f32[256,128]{1,0:T(8,128)S(1)}, s32[]{:T(128)}, f32[32,256,128]{2,1,0:T(8,128)}, s32[]{:T(128)}, /*index=5*/s32[]{:T(128)}) while((s32[]{:T(128)}, f32[256,128]{1,0:T(8,128)S(1)}, s32[]{:T(128)}, f32[32,256,128]{2,1,0:T(8,128)}, s32[]{:T(128)}, /*index=5*/s32[]{:T(128)}) %tuple.227), condition=%wide.region_24.27_spmd.clone, body=%wide.region_23.26_spmd.clone.sunk | while | flops 98308 | bytes 393309 | solution.py:19
  1374.0 1.6 copy.30
  1375.6 98.8 %all-reduce.2.cloned.1.call-done = f32[256,128]{1,0:T(8,128)} async-done(((f32[256,128]{1,0:T(8,128)}), f32[256,128]{1,0:T(8,128)}) %all-reduce.2.cloned.1.call-update) | async-done | bytes 131088 | tf_op jit(solution)/shard_map/psum | solution.py:24
  1474.4 1.6 broadcast_multiply_fusion
  (281 shorter events, 188.6 us)
Async XLA Ops:
  7.2 33.5 %copy-start = (f32[32,2048]{1,0:T(8,128)S(1)}, f32[32,2048]{1,0:T(8,128)}, u32[]{:S(2)}) copy-start(f32[32,2048]{1,0:T(8,128)} %param.21) | copy-start | bytes 786436
  10.4 30.3 %all-to-all-start = ((f32[256,4,512]{2,0,1:T(8,128)}), f32[256,4,512]{2,0,1:T(8,128)S(1)}, u32[]{:S(2)}, u32[]{:S(2)}) async-start(f32[256,4,512]{2,0,1:T(8,128)} %bitcast.156), calls=%async_computation | async-start | bytes 4194304 | tf_op jit(solution)/shard_map/all_to_all | solution.py:64
  15.2 48.3 %reduce-scatter.7.cloned.1.call-start = ((), (), s32[]{:S(2)}) async-start(), calls=%async_computation.8 | async-start | bytes 163840 | tf_op jit(solution)/shard_map/reduce_scatter | solution.py:47
  43.4 67.8 %all-gather.13.cloned.1.call-start = ((), (), s32[]{:S(2)}) async-start(), calls=%async_computation.15 | async-start | bytes 1081344 | tf_op jit(solution)/shard_map/all_gather | solution.py:12
  63.5 245.0 %reduce-scatter.9.cloned.1.call-start = ((), (), s32[]{:S(2)}) async-start(), calls=%async_computation.9 | async-start | bytes 163840 | tf_op jit(solution)/shard_map/reduce_scatter | solution.py:47
  114.7 30.1 %copy-start.3 = (f32[256,32]{0,1:T(8,128)S(1)}, f32[256,32]{0,1:T(8,128)}, u32[]{:S(2)}) copy-start(f32[256,32]{0,1:T(8,128)} %reduce-scatter.7.cloned.1.call-done) | copy-start | bytes 98308
  286.8 69.2 %all-gather.15.cloned.1.call-start = ((), (), s32[]{:S(2)}) async-start(), calls=%async_computation.16 | async-start | bytes 1081344 | tf_op jit(solution)/shard_map/all_gather | solution.py:12
  308.5 244.8 %reduce-scatter.11.cloned.1.call-start = ((), (), s32[]{:S(2)}) async-start(), calls=%async_computation.10 | async-start | bytes 163840 | tf_op jit(solution)/shard_map/reduce_scatter | solution.py:47
  359.5 30.1 %copy-start.5 = (f32[256,32]{0,1:T(8,128)S(1)}, f32[256,32]{0,1:T(8,128)}, u32[]{:S(2)}) copy-start(f32[256,32]{0,1:T(8,128)} %reduce-scatter.9.cloned.1.call-done) | copy-start | bytes 98308
  531.6 69.2 %all-gather.17.cloned.1.call-start = ((), (), s32[]{:S(2)}) async-start(), calls=%async_computation.17 | async-start | bytes 1081344 | tf_op jit(solution)/shard_map/all_gather | solution.py:12
  553.3 245.0 %reduce-scatter.13.cloned.1.call-start = ((), (), s32[]{:S(2)}) async-start(), calls=%async_computation.11 | async-start | bytes 163840 | tf_op jit(solution)/shard_map/reduce_scatter | solution.py:47
  604.3 30.1 %copy-start.6 = (f32[256,32]{0,1:T(8,128)S(1)}, f32[256,32]{0,1:T(8,128)}, u32[]{:S(2)}) copy-start(f32[256,32]{0,1:T(8,128)} %reduce-scatter.11.cloned.1.call-done) | copy-start | bytes 98308
  776.6 69.3 %all-gather.19.cloned.1.call-start = ((), (), s32[]{:S(2)}) async-start(), calls=%async_computation.18 | async-start | bytes 1081344 | tf_op jit(solution)/shard_map/all_gather | solution.py:12
  798.3 244.9 %reduce-scatter.15.cloned.1.call-start = ((), (), s32[]{:S(2)}) async-start(), calls=%async_computation.12 | async-start | bytes 163840 | tf_op jit(solution)/shard_map/reduce_scatter | solution.py:47
  849.5 30.1 %copy-start.7 = (f32[256,32]{0,1:T(8,128)S(1)}, f32[256,32]{0,1:T(8,128)}, u32[]{:S(2)}) copy-start(f32[256,32]{0,1:T(8,128)} %reduce-scatter.13.cloned.1.call-done) | copy-start | bytes 98308
  1021.6 69.1 %all-gather.21.cloned.1.call-start = ((), (), s32[]{:S(2)}) async-start(), calls=%async_computation.19 | async-start | bytes 1081344 | tf_op jit(solution)/shard_map/all_gather | solution.py:12
  1043.3 249.1 %reduce-scatter.17.cloned.1.call-start = ((), (), s32[]{:S(2)}) async-start(), calls=%async_computation.13 | async-start | bytes 655360 | tf_op jit(solution)/shard_map/reduce_scatter | solution.py:47
  1094.3 30.1 %copy-start.4 = (f32[256,32]{0,1:T(8,128)S(1)}, f32[256,32]{0,1:T(8,128)}, u32[]{:S(2)}) copy-start(f32[256,32]{0,1:T(8,128)} %reduce-scatter.15.cloned.1.call-done) | copy-start | bytes 98308
  1265.7 1.3 copy-start.1
  1269.8 73.5 %all-gather.23.cloned.1.call-start = ((), (), s32[]{:S(2)}) async-start(), calls=%async_computation.20 | async-start | bytes 4325376 | tf_op jit(solution)/shard_map/all_gather | solution.py:12
  1292.4 81.6 %all-to-all-start.1 = ((f32[4,256,512]{2,1,0:T(8,128)}), f32[4,256,512]{2,1,0:T(8,128)S(1)}, u32[]{:S(2)}, u32[]{:S(2)}) async-start(f32[4,256,512]{2,1,0:T(8,128)} %bitcast.154), calls=%async_computation.6 | async-start | bytes 4194304 | tf_op jit(solution)/shard_map/all_to_all | solution.py:78
  1296.1 77.2 %copy-start.2 = (f32[256,128]{1,0:T(8,128)S(1)}, f32[256,128]{1,0:T(8,128)}, u32[]{:S(2)}) copy-start(f32[256,128]{1,0:T(8,128)} %reduce-scatter.17.cloned.1.call-done) | copy-start | bytes 393220
  1296.1 178.3 %all-reduce.2.cloned.1.call-start = ((), (), s32[]{:S(2)}) async-start(), calls=%async_computation.14 | async-start | bytes 262144 | tf_op jit(solution)/shard_map/psum | solution.py:24
Sparse Core Ops, SparseCore 0:
  43.5 19.9 reduce-scatter.6
  65.7 45.4 all-gather.12
  286.9 21.5 reduce-scatter.8
  310.5 45.4 all-gather.14
  531.7 21.5 reduce-scatter.10
  555.3 45.4 all-gather.16
  776.7 21.5 reduce-scatter.12
  800.5 45.3 all-gather.18
  1021.7 21.5 reduce-scatter.14
  1045.3 45.3 all-gather.20
  1269.9 22.4 reduce-scatter.16
  1294.5 48.6 all-gather.22
  1374.1 100.2 all-reduce.1
where the time goes:
time: 1490 us; the launch traced here: 1480 us
  blocking collectives  653 us (44%)
  waiting for transfers between devices  537 us (36%)
  other arithmetic  213 us (14%)
  matrix products  27.3 us (2%)
  local copies, waits for them, and re-layouts  25.4 us (2%)
    psum x5, blocking collectives, broadcast(): return lax.psum(kept, axis)  604 us
    all_gather x6, waiting for transfers between devices, prefix(): pieces = lax.all_gather(value, axis)  283 us
    select_n x186, other arithmetic, lap(): return jnp.where(position < mine, longer, total)  176 us
    reduce_scatter x6, waiting for transfers between devices, fold_freq(): return lax.psum_scatter(term, 'freq', scatter_dimension=0, tiled=True)  129 us
    psum x1, waiting for transfers between devices, broadcast(): return lax.psum(kept, axis)  98.8 us
    all_gather x5, blocking collectives, gather_rows(): return lax.all_gather(term, 'freq', axis=0, tiled=True)  48.9 us
  transfers between devices with their start and end apart: 15, of which 14 were waited for; matrix products, arithmetic and copies ran while one was open for 2% of the time, Pallas kernels for 0%

commit v1 on v0

--- a/solution.py
+++ b/solution.py
@@ -48,7 +48,15 @@
 
 
 def gather_rows(term):
-    return lax.all_gather(term, "freq", axis=0, tiled=True)
+
+    def lines_mark(s0, peer_axis):
+        all_rows = jax.lax.psum(1, peer_axis)
+        back = jnp.stack([s0] * all_rows, axis=0)
+        return jnp.concatenate(
+            jax.lax.all_to_all(back, axis_name=peer_axis, split_axis=0, concat_axis=0), axis=0
+        )
+
+    return lines_mark(term, "freq")
 
 
 def slice_table(slices, weights):

time: 1490 us -> 1470 us (0.987)
    all_gather x5 -> x0, blocking collectives: 48.9 us -> none  [gather_rows(): return lax.all_gather(term, 'freq', axis=0, tiled=True)]
    all_to_all x0 -> x4, blocking collectives: none -> 34.4 us  [lines_mark(): jax.lax.all_to_all(back, axis_name=peer_axis, split_axis=0, concat_axis=0)]
  transfers between devices with their start and end apart: 15 -> 16, of which waited for: 14 -> 15; matrix products, arithmetic and copies ran while one was open for 2% -> 2% of each run, Pallas kernels for 0% -> 0%
where the time goes in v1:
time: 1470 us
  blocking collectives  639 us (43%)
  waiting for transfers between devices  530 us (36%)
  other arithmetic  213 us (14%)
  matrix products  27.1 us (2%)
  local copies, waits for them, and re-layouts  26.3 us (2%)
    psum x5, blocking collectives, broadcast(): return lax.psum(kept, axis)  604 us
    all_gather x6, waiting for transfers between devices, prefix(): pieces = lax.all_gather(value, axis)  284 us
    select_n x186, other arithmetic, lap(): return jnp.where(position < mine, longer, total)  176 us
    reduce_scatter x6, waiting for transfers between devices, fold_freq(): return lax.psum_scatter(term, 'freq', scatter_dimension=0, tiled=True)  117 us
    psum x1, waiting for transfers between devices, broadcast(): return lax.psum(kept, axis)  98.8 us
    all_to_all x4, blocking collectives, lines_mark(): jax.lax.all_to_all(back, axis_name=peer_axis, split_axis=0, concat_axis=0)  34.4 us
  transfers between devices with their start and end apart: 16, of which 15 were waited for; matrix products, arithmetic and copies ran while one was open for 2% of the time, Pallas kernels for 0%

profile of v1, /device:TPU:1, one launch (start us, length us, event | category | flops | bytes accessed | tf_op | source)
XLA Modules:
  0.0 1465.7 jit_solution(13363620796860672328)
XLA Ops:
  7.2 3.2 copy.59
  10.4 4.8 all-to-all-start
  15.2 25.5 %all-to-all-done = f32[256,4,512]{2,0,1:T(8,128)S(1)} async-done(((f32[256,4,512]{2,0,1:T(8,128)}), f32[256,4,512]{2,0,1:T(8,128)S(1)}, u32[]{:S(2)}, u32[]{:S(2)}) %all-to-all-start) | async-done | bytes 2097184 | tf_op jit(solution)/shard_map/all_to_all | solution.py:72
  40.7 2.7 convolution_bitcast_fusion.9
  43.4 20.1 %reduce-scatter.7.cloned.1.call-done = f32[256,32]{0,1:T(8,128)} async-done(((f32[1024,32]{0,1:T(8,128)}), f32[256,32]{0,1:T(8,128)}) %reduce-scatter.7.cloned.1.call-update) | async-done | bytes 32784 | tf_op jit(solution)/shard_map/reduce_scatter | solution.py:47
  63.6 47.6 %all-gather.13.cloned.1.call-done = f32[8192,32]{0,1:T(8,128)} async-done(((f32[256,32]{0,1:T(8,128)}), f32[8192,32]{0,1:T(8,128)}) %all-gather.13.cloned.1.call-update) | async-done | bytes 1048592 | tf_op jit(solution)/shard_map/all_gather | solution.py:12
  111.1 3.6 copy.46
  114.7 30.1 %while.84 = (s32[]{:T(128)}, f32[256,32]{1,0:T(8,128)S(1)}, s32[]{:T(128)}, f32[32,256,32]{2,1,0:T(8,128)}, s32[]{:T(128)}, /*index=5*/s32[]{:T(128)}) while((s32[]{:T(128)}, f32[256,32]{1,0:T(8,128)S(1)}, s32[]{:T(128)}, f32[32,256,32]{2,1,0:T(8,128)}, s32[]{:T(128)}, /*index=5*/s32[]{:T(128)}) %tuple.227), condition=%wide.region_2.3_spmd.clone, body=%wide.region_1.2_spmd.clone.sunk | while | flops 24580 | bytes 98397 | solution.py:19
  144.9 120.9 %psum.42 = f32[256,32]{0,1:T(8,128)S(1)} all-reduce(f32[256,32]{0,1:T(8,128)S(1)} %add_select_fusion.11), channel_id=1, replica_groups=mesh['pix'=32,'freq'=4] {'pix'}, use_global_device_ids=true, to_apply=%region_3.4 | all-reduce | flops 8192 | bytes 65536 | tf_op jit(solution)/shard_map/psum | solution.py:24
  265.7 8.6 all_to_all.63
  274.7 2.9 cholesky.89
  278.9 2.4 custom-call.15
  281.7 1.3 fusion.31
  283.0 2.7 convolution_bitcast_fusion.7
  285.8 19.3 %reduce-scatter.9.cloned.1.call-done = f32[256,32]{0,1:T(8,128)} async-done(((f32[1024,32]{0,1:T(8,128)}), f32[256,32]{0,1:T(8,128)}) %reduce-scatter.9.cloned.1.call-update) | async-done | bytes 32784 | tf_op jit(solution)/shard_map/reduce_scatter | solution.py:47
  305.1 47.4 %all-gather.15.cloned.1.call-done = f32[8192,32]{0,1:T(8,128)} async-done(((f32[256,32]{0,1:T(8,128)}), f32[8192,32]{0,1:T(8,128)}) %all-gather.15.cloned.1.call-update) | async-done | bytes 1048592 | tf_op jit(solution)/shard_map/all_gather | solution.py:12
  352.5 3.6 copy.47
  356.1 30.1 %while.85 = (s32[]{:T(128)}, f32[256,32]{1,0:T(8,128)S(1)}, s32[]{:T(128)}, f32[32,256,32]{2,1,0:T(8,128)}, s32[]{:T(128)}, /*index=5*/s32[]{:T(128)}) while((s32[]{:T(128)}, f32[256,32]{1,0:T(8,128)S(1)}, s32[]{:T(128)}, f32[32,256,32]{2,1,0:T(8,128)}, s32[]{:T(128)}, /*index=5*/s32[]{:T(128)}) %tuple.228), condition=%wide.region_8.11_spmd.clone, body=%wide.region_7.10_spmd.clone.sunk | while | flops 24580 | bytes 98397 | solution.py:19
  386.2 120.9 %psum.43 = f32[256,32]{0,1:T(8,128)S(1)} all-reduce(f32[256,32]{0,1:T(8,128)S(1)} %add_select_fusion.10), channel_id=1, replica_groups=mesh['pix'=32,'freq'=4] {'pix'}, use_global_device_ids=true, to_apply=%region_9.12 | all-reduce | flops 8192 | bytes 65536 | tf_op jit(solution)/shard_map/psum | solution.py:24
  507.1 8.6 all_to_all.64
  516.1 2.9 cholesky.100
  520.3 2.4 custom-call.16
  523.1 1.3 fusion.32
  524.4 2.7 convolution_bitcast_fusion.5
  527.1 19.3 %reduce-scatter.11.cloned.1.call-done = f32[256,32]{0,1:T(8,128)} async-done(((f32[1024,32]{0,1:T(8,128)}), f32[256,32]{0,1:T(8,128)}) %reduce-scatter.11.cloned.1.call-update) | async-done | bytes 32784 | tf_op jit(solution)/shard_map/reduce_scatter | solution.py:47
  546.5 47.4 %all-gather.17.cloned.1.call-done = f32[8192,32]{0,1:T(8,128)} async-done(((f32[256,32]{0,1:T(8,128)}), f32[8192,32]{0,1:T(8,128)}) %all-gather.17.cloned.1.call-update) | async-done | bytes 1048592 | tf_op jit(solution)/shard_map/all_gather | solution.py:12
  593.9 3.6 copy.48
  597.5 30.1 %while.86 = (s32[]{:T(128)}, f32[256,32]{1,0:T(8,128)S(1)}, s32[]{:T(128)}, f32[32,256,32]{2,1,0:T(8,128)}, s32[]{:T(128)}, /*index=5*/s32[]{:T(128)}) while((s32[]{:T(128)}, f32[256,32]{1,0:T(8,128)S(1)}, s32[]{:T(128)}, f32[32,256,32]{2,1,0:T(8,128)}, s32[]{:T(128)}, /*index=5*/s32[]{:T(128)}) %tuple.229), condition=%wide.region_12.15_spmd.clone, body=%wide.region_11.14_spmd.clone.sunk | while | flops 24580 | bytes 98397 | solution.py:19
  627.6 120.9 %psum.44 = f32[256,32]{0,1:T(8,128)S(1)} all-reduce(f32[256,32]{0,1:T(8,128)S(1)} %add_select_fusion.9), channel_id=1, replica_groups=mesh['pix'=32,'freq'=4] {'pix'}, use_global_device_ids=true, to_apply=%region_13.16 | all-reduce | flops 8192 | bytes 65536 | tf_op jit(solution)/shard_map/psum | solution.py:24
  748.5 8.6 all_to_all.65
  757.5 2.9 cholesky.111
  761.7 2.4 custom-call.17
  764.5 1.3 fusion.33
  765.8 2.7 convolution_bitcast_fusion.3
  768.6 19.2 %reduce-scatter.13.cloned.1.call-done = f32[256,32]{0,1:T(8,128)} async-done(((f32[1024,32]{0,1:T(8,128)}), f32[256,32]{0,1:T(8,128)}) %reduce-scatter.13.cloned.1.call-update) | async-done | bytes 32784 | tf_op jit(solution)/shard_map/reduce_scatter | solution.py:47
  787.9 47.5 %all-gather.19.cloned.1.call-done = f32[8192,32]{0,1:T(8,128)} async-done(((f32[256,32]{0,1:T(8,128)}), f32[8192,32]{0,1:T(8,128)}) %all-gather.19.cloned.1.call-update) | async-done | bytes 1048592 | tf_op jit(solution)/shard_map/all_gather | solution.py:12
  835.4 3.6 copy.49
  839.0 30.1 %while.87 = (s32[]{:T(128)}, f32[256,32]{1,0:T(8,128)S(1)}, s32[]{:T(128)}, f32[32,256,32]{2,1,0:T(8,128)}, s32[]{:T(128)}, /*index=5*/s32[]{:T(128)}) while((s32[]{:T(128)}, f32[256,32]{1,0:T(8,128)S(1)}, s32[]{:T(128)}, f32[32,256,32]{2,1,0:T(8,128)}, s32[]{:T(128)}, /*index=5*/s32[]{:T(128)}) %tuple.230), condition=%wide.region_16.19_spmd.clone, body=%wide.region_15.18_spmd.clone.sunk | while | flops 24580 | bytes 98397 | solution.py:19
  869.1 120.9 %psum.45 = f32[256,32]{0,1:T(8,128)S(1)} all-reduce(f32[256,32]{0,1:T(8,128)S(1)} %add_select_fusion.8), channel_id=1, replica_groups=mesh['pix'=32,'freq'=4] {'pix'}, use_global_device_ids=true, to_apply=%region_17.20 | all-reduce | flops 8192 | bytes 65536 | tf_op jit(solution)/shard_map/psum | solution.py:24
  990.0 8.6 all_to_all.66
  998.9 2.9 cholesky.122
  1003.2 2.4 custom-call.18
  1006.0 1.3 fusion.34
  1007.3 2.7 convolution_bitcast_fusion.1
  1010.0 19.3 %reduce-scatter.15.cloned.1.call-done = f32[256,32]{0,1:T(8,128)} async-done(((f32[1024,32]{0,1:T(8,128)}), f32[256,32]{0,1:T(8,128)}) %reduce-scatter.15.cloned.1.call-update) | async-done | bytes 32784 | tf_op jit(solution)/shard_map/reduce_scatter | solution.py:47
  1030.1 46.6 %all-gather.21.cloned.1.call-done = f32[8192,32]{0,1:T(8,128)} async-done(((f32[256,32]{0,1:T(8,128)}), f32[8192,32]{0,1:T(8,128)}) %all-gather.21.cloned.1.call-update) | async-done | bytes 1048592 | tf_op jit(solution)/shard_map/all_gather | solution.py:12
  1076.7 3.6 copy.50
  1080.3 30.1 %while.88 = (s32[]{:T(128)}, f32[256,32]{1,0:T(8,128)S(1)}, s32[]{:T(128)}, f32[32,256,32]{2,1,0:T(8,128)}, s32[]{:T(128)}, /*index=5*/s32[]{:T(128)}) while((s32[]{:T(128)}, f32[256,32]{1,0:T(8,128)S(1)}, s32[]{:T(128)}, f32[32,256,32]{2,1,0:T(8,128)}, s32[]{:T(128)}, /*index=5*/s32[]{:T(128)}) %tuple.231), condition=%wide.region_20.23_spmd.clone, body=%wide.region_19.22_spmd.clone.sunk | while | flops 24580 | bytes 98397 | solution.py:19
  1110.5 120.9 %psum.46 = f32[256,32]{0,1:T(8,128)S(1)} all-reduce(f32[256,32]{0,1:T(8,128)S(1)} %add_select_fusion.7), channel_id=1, replica_groups=mesh['pix'=32,'freq'=4] {'pix'}, use_global_device_ids=true, to_apply=%region_21.24 | all-reduce | flops 8192 | bytes 65536 | tf_op jit(solution)/shard_map/psum | solution.py:24
  1232.0 4.0 all-to-all-start.5
  1236.8 4.0 all-to-all-done.5
  1241.1 2.9 cholesky.133
  1245.4 2.4 custom-call.19
  1248.2 1.3 fusion.35
  1249.5 1.8 convolution_subtract_fusion
  1251.4 1.3 copy-done.1
  1252.7 2.7 fusion
  1255.4 20.2 %reduce-scatter.17.cloned.1.call-done = f32[256,128]{1,0:T(8,128)} async-done(((f32[1024,128]{1,0:T(8,128)}), f32[256,128]{1,0:T(8,128)}) %reduce-scatter.17.cloned.1.call-update) | async-done | bytes 131088 | tf_op jit(solution)/shard_map/reduce_scatter | solution.py:47
  1275.7 3.6 all-to-all-start.6
  1279.3 47.1 %all-gather.23.cloned.1.call-done = f32[8192,128]{1,0:T(8,128)} async-done(((f32[256,128]{1,0:T(8,128)}), f32[8192,128]{1,0:T(8,128)}) %all-gather.23.cloned.1.call-update) | async-done | bytes 4194320 | tf_op jit(solution)/shard_map/all_gather | solution.py:12
  1326.5 30.0 %while.89 = (s32[]{:T(128)}, f32[256,128]{1,0:T(8,128)S(1)}, s32[]{:T(128)}, f32[32,256,128]{2,1,0:T(8,128)}, s32[]{:T(128)}, /*index=5*/s32[]{:T(128)}) while((s32[]{:T(128)}, f32[256,128]{1,0:T(8,128)S(1)}, s32[]{:T(128)}, f32[32,256,128]{2,1,0:T(8,128)}, s32[]{:T(128)}, /*index=5*/s32[]{:T(128)}) %tuple.232), condition=%wide.region_24.27_spmd.clone, body=%wide.region_23.26_spmd.clone.sunk | while | flops 98308 | bytes 393309 | solution.py:19
  1357.2 1.6 copy.57
  1358.8 98.8 %all-reduce.2.cloned.1.call-done = f32[256,128]{1,0:T(8,128)} async-done(((f32[256,128]{1,0:T(8,128)}), f32[256,128]{1,0:T(8,128)}) %all-reduce.2.cloned.1.call-update) | async-done | bytes 131088 | tf_op jit(solution)/shard_map/psum | solution.py:24
  1457.6 1.6 broadcast_multiply_fusion
  (292 shorter events, 190.2 us)
Async XLA Ops:
  7.2 33.5 %copy-start = (f32[32,2048]{1,0:T(8,128)S(1)}, f32[32,2048]{1,0:T(8,128)}, u32[]{:S(2)}) copy-start(f32[32,2048]{1,0:T(8,128)} %param.21) | copy-start | bytes 786436
  10.4 30.3 %all-to-all-start = ((f32[256,4,512]{2,0,1:T(8,128)}), f32[256,4,512]{2,0,1:T(8,128)S(1)}, u32[]{:S(2)}, u32[]{:S(2)}) async-start(f32[256,4,512]{2,0,1:T(8,128)} %bitcast.176), calls=%async_computation | async-start | bytes 4194304 | tf_op jit(solution)/shard_map/all_to_all | solution.py:72
  15.2 48.3 %reduce-scatter.7.cloned.1.call-start = ((), (), s32[]{:S(2)}) async-start(), calls=%async_computation.13 | async-start | bytes 163840 | tf_op jit(solution)/shard_map/reduce_scatter | solution.py:47
  43.4 67.8 %all-gather.13.cloned.1.call-start = ((), (), s32[]{:S(2)}) async-start(), calls=%async_computation.20 | async-start | bytes 1081344 | tf_op jit(solution)/shard_map/all_gather | solution.py:12
  63.5 241.5 %reduce-scatter.9.cloned.1.call-start = ((), (), s32[]{:S(2)}) async-start(), calls=%async_computation.14 | async-start | bytes 163840 | tf_op jit(solution)/shard_map/reduce_scatter | solution.py:47
  114.7 30.1 %copy-start.3 = (f32[256,32]{0,1:T(8,128)S(1)}, f32[256,32]{0,1:T(8,128)}, u32[]{:S(2)}) copy-start(f32[256,32]{0,1:T(8,128)} %reduce-scatter.7.cloned.1.call-done) | copy-start | bytes 98308
  285.7 66.8 %all-gather.15.cloned.1.call-start = ((), (), s32[]{:S(2)}) async-start(), calls=%async_computation.21 | async-start | bytes 1081344 | tf_op jit(solution)/shard_map/all_gather | solution.py:12
  305.1 241.4 %reduce-scatter.11.cloned.1.call-start = ((), (), s32[]{:S(2)}) async-start(), calls=%async_computation.15 | async-start | bytes 163840 | tf_op jit(solution)/shard_map/reduce_scatter | solution.py:47
  356.1 30.1 %copy-start.4 = (f32[256,32]{0,1:T(8,128)S(1)}, f32[256,32]{0,1:T(8,128)}, u32[]{:S(2)}) copy-start(f32[256,32]{0,1:T(8,128)} %reduce-scatter.9.cloned.1.call-done) | copy-start | bytes 98308
  527.1 66.8 %all-gather.17.cloned.1.call-start = ((), (), s32[]{:S(2)}) async-start(), calls=%async_computation.22 | async-start | bytes 1081344 | tf_op jit(solution)/shard_map/all_gather | solution.py:12
  546.4 241.4 %reduce-scatter.13.cloned.1.call-start = ((), (), s32[]{:S(2)}) async-start(), calls=%async_computation.16 | async-start | bytes 163840 | tf_op jit(solution)/shard_map/reduce_scatter | solution.py:47
  597.5 30.1 %copy-start.5 = (f32[256,32]{0,1:T(8,128)S(1)}, f32[256,32]{0,1:T(8,128)}, u32[]{:S(2)}) copy-start(f32[256,32]{0,1:T(8,128)} %reduce-scatter.11.cloned.1.call-done) | copy-start | bytes 98308
  768.5 66.9 %all-gather.19.cloned.1.call-start = ((), (), s32[]{:S(2)}) async-start(), calls=%async_computation.23 | async-start | bytes 1081344 | tf_op jit(solution)/shard_map/all_gather | solution.py:12
  787.8 241.5 %reduce-scatter.15.cloned.1.call-start = ((), (), s32[]{:S(2)}) async-start(), calls=%async_computation.17 | async-start | bytes 163840 | tf_op jit(solution)/shard_map/reduce_scatter | solution.py:47
  839.0 30.1 %copy-start.6 = (f32[256,32]{0,1:T(8,128)S(1)}, f32[256,32]{0,1:T(8,128)}, u32[]{:S(2)}) copy-start(f32[256,32]{0,1:T(8,128)} %reduce-scatter.13.cloned.1.call-done) | copy-start | bytes 98308
  1010.0 66.8 %all-gather.21.cloned.1.call-start = ((), (), s32[]{:S(2)}) async-start(), calls=%async_computation.24 | async-start | bytes 1081344 | tf_op jit(solution)/shard_map/all_gather | solution.py:12
  1080.3 30.1 %copy-start.7 = (f32[256,32]{0,1:T(8,128)S(1)}, f32[256,32]{0,1:T(8,128)}, u32[]{:S(2)}) copy-start(f32[256,32]{0,1:T(8,128)} %reduce-scatter.15.cloned.1.call-done) | copy-start | bytes 98308
  1232.0 8.8 all-to-all-start.5
  1236.0 39.6 %reduce-scatter.17.cloned.1.call-start = ((), (), s32[]{:S(2)}) async-start(), calls=%async_computation.18 | async-start | bytes 655360 | tf_op jit(solution)/shard_map/reduce_scatter | solution.py:47
  1251.3 1.3 copy-start.1
  1255.4 71.1 %all-gather.23.cloned.1.call-start = ((), (), s32[]{:S(2)}) async-start(), calls=%async_computation.25 | async-start | bytes 4325376 | tf_op jit(solution)/shard_map/all_gather | solution.py:12
  1275.7 81.6 %all-to-all-start.6 = ((f32[4,256,512]{2,1,0:T(8,128)}), f32[4,256,512]{2,1,0:T(8,128)S(1)}, u32[]{:S(2)}, u32[]{:S(2)}) async-start(f32[4,256,512]{2,1,0:T(8,128)} %bitcast.174), calls=%async_computation.11 | async-start | bytes 4194304 | tf_op jit(solution)/shard_map/all_to_all | solution.py:86
  1279.3 77.2 %copy-start.2 = (f32[256,128]{1,0:T(8,128)S(1)}, f32[256,128]{1,0:T(8,128)}, u32[]{:S(2)}) copy-start(f32[256,128]{1,0:T(8,128)} %reduce-scatter.17.cloned.1.call-done) | copy-start | bytes 393220
  1279.3 178.3 %all-reduce.2.cloned.1.call-start = ((), (), s32[]{:S(2)}) async-start(), calls=%async_computation.19 | async-start | bytes 262144 | tf_op jit(solution)/shard_map/psum | solution.py:24
Sparse Core Ops, SparseCore 0:
  43.5 19.9 reduce-scatter.6
  65.7 45.4 all-gather.12
  285.8 19.1 reduce-scatter.8
  307.1 45.3 all-gather.14
  527.2 19.1 reduce-scatter.10
  548.5 45.4 all-gather.16
  768.6 19.1 reduce-scatter.12
  790.0 45.3 all-gather.18
  1010.1 19.1 reduce-scatter.14
  1031.3 45.3 all-gather.20
  1255.5 20.0 reduce-scatter.16
  1277.7 48.6 all-gather.22
  1357.3 100.2 all-reduce.1
